TPU v7x, 32 devices: a whole 2x2x4 slice. The times are simulated.
32 devices in a mesh: ep: 8 (over z, x), tp: 4 (over y, core).
Axes of the slice: x: 2, y: 2, z: 4, core: 2. Of those that a mesh axis runs over, the one named last changes fastest.
Arguments:
- tokens: bfloat16 [2, 128, 4096], P(None, 'ep'), may hold values from -6 to 6
- route_ids: int32 [2, 128, 8], P(None, 'ep'), may hold values from 0 to 15, all different within a row; in each aligned block of 16 rows (0 to 15, 16 to 31, ..., all dimensions but the last counted through in order) at most 10 rows name the same one
- route_weights: float32 [2, 128, 8], P(None, 'ep'), may hold values from 0.1 to 0.4
- train_map: int32 [64], replicated, may hold values from 0 to 63, each once
- serve_place: int32 [64], replicated, may hold values from 0 to 15, as said below
- train_gate: bfloat16 [64, 1024, 1536], P('ep', None, 'tp'), may hold values from -0.09375 to 0.09375
- train_up: bfloat16 [64, 1024, 1536], P('ep', None, 'tp'), may hold values from -0.09375 to 0.09375
- train_down: bfloat16 [64, 1024, 1536], P('ep', None, 'tp'), may hold values from -0.15625 to 0.15625
Outputs:
- serve_gate: bfloat16 [64, 4096, 1536], P('ep', None, 'tp')
- serve_up: bfloat16 [64, 4096, 1536], P('ep', None, 'tp')
- serve_down: bfloat16 [64, 4096, 1536], P('ep', None, 'tp')
- moe_out: bfloat16 [2, 128, 4096], P(None, 'ep', 'tp')
Inputs may be any that keep to these rules, and one draw needn't show every extreme that they name: `route_ids`: each row names 8 different experts; in each aligned block of 16 rows (one index of ep in one step) no expert is named by more than 10 rows. `train_map`: each trainer slot holds a different piece; piece q is part q % 4 of expert q // 4. `serve_place`: every expert occupies two or more serving slots, and some expert exactly two.
All inputs are finite; a program needn't handle non-finite values.
Results may differ from a plain program's by a relative error of at most 0.012.
Values may be sent and summed in bfloat16 or wider, within the bound.
A program may use at most 256 MiB of HBM per device.

v0:
```python
import jax
import jax.numpy as jnp
from jax import lax
from jax.sharding import PartitionSpec as P

EXPERTS = 16
MOST = 10


def body(
    tokens, route_ids, route_weights, train_map, serve_place, train_gate, train_up, train_down
):
    ep_count = lax.axis_size("ep")
    tp_count = lax.axis_size("tp")
    slot_count = serve_place.shape[0]
    local_slots = train_gate.shape[0]
    part_count = slot_count // EXPERTS
    piece_rows = train_gate.shape[1]
    quarter_width = train_gate.shape[2]
    block_rows = piece_rows // ep_count
    block_gate, block_up, block_down = (
        lax.all_to_all(train_gate, "ep", split_axis=1, concat_axis=0, tiled=True),
        lax.all_to_all(train_up, "ep", split_axis=1, concat_axis=0, tiled=True),
        lax.all_to_all(train_down, "ep", split_axis=1, concat_axis=0, tiled=True),
    )
    slot_iota = jnp.arange(slot_count, dtype=jnp.int32)
    inverse = jnp.sum(
        jnp.where(train_map[:, None] == slot_iota[None, :], slot_iota[:, None], 0), axis=0
    )
    wanted = (
        serve_place[:, None] * part_count + jnp.arange(part_count, dtype=jnp.int32)[None, :]
    ).reshape(-1)
    source_slot = jnp.take(inverse, wanted)

    def select_pieces(blocks):
        return jnp.take(blocks, source_slot, axis=0).reshape(
            slot_count, part_count, block_rows, quarter_width
        )

    arrived_gate, arrived_up, arrived_down = (
        lax.all_to_all(select_pieces(block_gate), "ep", split_axis=0, concat_axis=2, tiled=True),
        lax.all_to_all(select_pieces(block_up), "ep", split_axis=0, concat_axis=2, tiled=True),
        lax.all_to_all(select_pieces(block_down), "ep", split_axis=0, concat_axis=2, tiled=True),
    )
    model_rows = part_count * piece_rows
    serve_gate = arrived_gate.reshape(local_slots, model_rows, quarter_width)
    serve_up = arrived_up.reshape(local_slots, model_rows, quarter_width)
    serve_down = arrived_down.reshape(local_slots, model_rows, quarter_width)
    ep_index = lax.axis_index("ep")
    tok_count = tokens.shape[1]
    topk_count = route_ids.shape[2]
    pair_count = tok_count * topk_count
    same_slot = serve_place[:, None] == serve_place[None, :]
    replica_rank = jnp.sum(same_slot & (slot_iota[None, :] < slot_iota[:, None]), axis=1)
    pair_iota = jnp.arange(pair_count, dtype=jnp.int32)
    model_width = tokens.shape[2]
    out_width = model_width // tp_count
    results = []
    for decode_step in range(tokens.shape[0]):
        pair_experts = route_ids[decode_step].reshape(pair_count)
        holders = serve_place[None, :] == pair_experts[:, None]
        replica_count = jnp.sum(holders, axis=1)
        earlier_pairs = (pair_experts[:, None] == pair_experts[None, :]) & (
            pair_iota[None, :] < pair_iota[:, None]
        )
        seen = jnp.sum(earlier_pairs, axis=1)
        target = (seen + ep_index) % replica_count
        position = seen // replica_count
        capacity = (MOST + 1) // 2
        chosen = holders & (replica_rank[None, :] == target[:, None])
        dest_slot = jnp.sum(jnp.where(chosen, slot_iota[None, :], 0), axis=1)
        row_index = dest_slot * capacity + position
        buffer_rows = slot_count * capacity
        placing = row_index[None, :] == jnp.arange(buffer_rows, dtype=jnp.int32)[:, None]
        placing = jnp.any(placing.reshape(buffer_rows, tok_count, topk_count), axis=2).astype(
            jnp.bfloat16
        )
        row_source = tokens[decode_step]
        send_rows = jnp.dot(placing, row_source, preferred_element_type=jnp.float32).astype(
            jnp.bfloat16
        )
        send_rows = send_rows.reshape(ep_count, local_slots, capacity, row_source.shape[1])
        received = lax.all_to_all(send_rows, "ep", split_axis=0, concat_axis=0, tiled=True)
        gate_act = jnp.einsum(
            "plmd,ldf->plmf", received, serve_gate, preferred_element_type=jnp.float32
        )
        up_act = jnp.einsum(
            "plmd,ldf->plmf", received, serve_up, preferred_element_type=jnp.float32
        )
        hidden = (jax.nn.silu(gate_act) * up_act).astype(jnp.bfloat16)
        partial_value = jnp.einsum(
            "plmf,ldf->plmd", hidden, serve_down, preferred_element_type=jnp.float32
        ).astype(jnp.bfloat16)
        partial_value = lax.optimization_barrier(partial_value)
        summed = lax.psum_scatter(
            partial_value.astype(jnp.float32).astype(jnp.bfloat16),
            "tp",
            scatter_dimension=3,
            tiled=True,
        )
        returned = lax.all_to_all(summed, "ep", split_axis=0, concat_axis=0, tiled=True)
        flat_out = returned.reshape(buffer_rows, out_width)
        gathered = (
            jnp.take(flat_out, row_index, axis=0)
            .astype(jnp.float32)
            .reshape(tok_count, topk_count, out_width)
        )
        mixed = jnp.sum(gathered * route_weights[decode_step][:, :, None], axis=1)
        results.append(mixed.astype(jnp.bfloat16))
    return (serve_gate, serve_up, serve_down, jnp.stack(results))


def solution(mesh):
    in_specs = (
        P(None, "ep", None),
        P(None, "ep", None),
        P(None, "ep", None),
        P(),
        P(),
        P("ep", None, "tp"),
        P("ep", None, "tp"),
        P("ep", None, "tp"),
    )
    out_specs = (P("ep", None, "tp"), P("ep", None, "tp"), P("ep", None, "tp"), P(None, "ep", "tp"))
    return jax.shard_map(body, mesh=mesh, in_specs=in_specs, out_specs=out_specs, check_vma=False)
```

profile of v0, /device:TPU:0, one launch (start us, length us, event | category | flops | bytes accessed | tf_op | source)
XLA Modules:
  0.0 2392.6 jit_solution(1493205404481428331)
XLA Ops:
  7.2 9.2 copy.98
  16.4 7.3 all-to-all-start.4
  23.6 9.2 copy.94
  32.8 129.0 %all-to-all-done.4 = bf16[8,1024,384]{2,0,1:T(8,128)(2,1)} async-done(((bf16[8,1024,384]{2,0,1:T(8,128)(2,1)}), bf16[8,1024,384]{2,0,1:T(8,128)(2,1)}, u32[]{:S(2)}, u32[]{:S(2)}) %all-to-all-start.4) | async-done | bytes 6291488 | tf_op jit(solution)/shard_map/all_to_all | solution.py:24
  167.1 9.1 copy.90
  176.2 128.2 %all-to-all-done.2 = bf16[8,1024,384]{2,0,1:T(8,128)(2,1)} async-done(((bf16[8,1024,384]{2,0,1:T(8,128)(2,1)}), bf16[8,1024,384]{2,0,1:T(8,128)(2,1)}, u32[]{:S(2)}, u32[]{:S(2)}) %all-to-all-start.2) | async-done | bytes 6291488 | tf_op jit(solution)/shard_map/all_to_all | solution.py:23
  311.5 6.9 copy.100
  318.4 6.9 copy.96
  325.3 16.0 gather_fusion.3
  341.3 16.0 gather_fusion.2
  357.3 89.1 %all-to-all-done = bf16[8,1024,384]{2,0,1:T(8,128)(2,1)} async-done(((bf16[8,1024,384]{2,0,1:T(8,128)(2,1)}), bf16[8,1024,384]{2,0,1:T(8,128)(2,1)}, u32[]{:S(2)}, u32[]{:S(2)}) %all-to-all-start) | async-done | bytes 6291488 | tf_op jit(solution)/shard_map/all_to_all | solution.py:22
  446.4 6.8 copy.92
  453.2 16.0 gather_fusion.1
  469.2 41.3 %broadcast_select_fusion = (bf16[256,128,384]{2,1,0:T(8,128)(2,1)}, bf16[256,128,384]{2,1,0:T(8,128)(2,1)S(1)}, bf16[256,128,384]{2,1,0:T(8,128)(2,1)}) fusion(bf16[256,128,384]{2,1,0:T(8,128)(2,1)} %gather_fusion.3, pred[256]{0:T(512)(128)(4,1)S(1)} %get-tuple-element.18, bf16[256,128,384]{2,1,0:T(8,128)(2,1)} %gather_fusion.2, ...), kind=kLoop, calls=%fused_computation.6 | loop fusion | flops 37748736 | bytes 150995200 | tf_op jit(solution)/shard_map/jit(_take)/select_n | solution.py:36
  510.5 551.4 %all_to_all.119 = bf16[64,4,128,384]{3,2,1,0:T(8,128)(2,1)} all-to-all(bf16[64,4,128,384]{3,2,1,0:T(8,128)(2,1)} %bitcast.104), channel_id=1, replica_groups=mesh['ep'=8,'tp'=4] {'ep'}, dimensions={0} | all-to-all | bytes 50331648 | tf_op jit(solution)/shard_map/all_to_all | solution.py:41
  1061.9 544.3 %all_to_all.120 = bf16[64,4,128,384]{3,2,1,0:T(8,128)(2,1)} all-to-all(bf16[64,4,128,384]{3,2,1,0:T(8,128)(2,1)S(1)} %bitcast.103), channel_id=1, replica_groups=mesh['ep'=8,'tp'=4] {'ep'}, dimensions={0} | all-to-all | bytes 50331648 | tf_op jit(solution)/shard_map/all_to_all | solution.py:42
  1606.2 6.7 all-to-all-start.5
  1624.7 529.3 %all-to-all-done.5 = bf16[64,4,128,384]{3,2,1,0:T(8,128)(2,1)} async-done(((bf16[64,4,128,384]{3,2,1,0:T(8,128)(2,1)}), bf16[64,4,128,384]{3,2,1,0:T(8,128)(2,1)}, u32[]{:S(2)}, u32[]{:S(2)}) %all-to-all-start.5) | async-done | bytes 25165856 | tf_op jit(solution)/shard_map/all_to_all | solution.py:43
  2162.5 5.7 copy.103
  2168.3 24.4 %copy.93 = bf16[8,4,8,128,384]{4,3,2,1,0:T(8,128)(2,1)} copy(bf16[8,4,8,128,384]{4,3,1,0,2:T(8,128)(2,1)} %bitcast.98) | data formatting | bytes 50331648 | tf_op jit(solution)/shard_map/all_to_all | solution.py:41
  2192.8 8.8 copy.97
  2201.6 21.0 copy.101
  2222.7 5.9 all-to-all-start.6
  2228.8 14.2 fusion.19
  2243.0 11.9 fusion.28
  2254.9 13.4 fusion.1
  2268.7 18.3 all-to-all-done.6
  2287.0 11.0 fusion.10
  2297.9 11.1 fusion.31
  2309.1 13.4 fusion
  2328.9 27.7 %reduce-scatter.3.cloned.1.call-done = bf16[8,8,5,1024]{3,0,2,1:T(8,128)(2,1)} async-done(((bf16[8,8,5,4096]{3,0,2,1:T(8,128)(2,1)}), bf16[8,8,5,1024]{3,0,2,1:T(8,128)(2,1)}) %reduce-scatter.3.cloned.1.call-update) | async-done | bytes 655376 | tf_op jit(solution)/shard_map/reduce_scatter | solution.py:95
  2365.4 16.3 all-to-all-done.7
  (98 shorter events, 51.8 us)
Async XLA Ops:
  16.4 145.5 %all-to-all-start.4 = ((bf16[8,1024,384]{2,0,1:T(8,128)(2,1)}), bf16[8,1024,384]{2,0,1:T(8,128)(2,1)}, u32[]{:S(2)}, u32[]{:S(2)}) async-start(bf16[8,1024,384]{2,0,1:T(8,128)(2,1)} %copy.98), calls=%async_computation.4 | async-start | bytes 12582912 | tf_op jit(solution)/shard_map/all_to_all | solution.py:24
  161.9 142.5 %all-to-all-start.2 = ((bf16[8,1024,384]{2,0,1:T(8,128)(2,1)}), bf16[8,1024,384]{2,0,1:T(8,128)(2,1)}, u32[]{:S(2)}, u32[]{:S(2)}) async-start(bf16[8,1024,384]{2,0,1:T(8,128)(2,1)} %copy.94), calls=%async_computation.2 | async-start | bytes 12582912 | tf_op jit(solution)/shard_map/all_to_all | solution.py:23
  176.2 132.9 %copy-start.7 = (s32[64]{0:T(128)S(1)}, s32[64]{0:T(128)}, u32[]{:S(2)}) copy-start(s32[64]{0:T(128)} %param.16) | copy-start | bytes 772
  176.2 133.3 %copy-start.8 = (s32[64]{0:T(128)S(1)}, s32[64]{0:T(128)}, u32[]{:S(2)}) copy-start(s32[64]{0:T(128)} %param.15) | copy-start | bytes 772
  304.4 142.0 %all-to-all-start = ((bf16[8,1024,384]{2,0,1:T(8,128)(2,1)}), bf16[8,1024,384]{2,0,1:T(8,128)(2,1)}, u32[]{:S(2)}, u32[]{:S(2)}) async-start(bf16[8,1024,384]{2,0,1:T(8,128)(2,1)} %copy.90), calls=%async_computation | async-start | bytes 12582912 | tf_op jit(solution)/shard_map/all_to_all | solution.py:22
  1606.2 6.7 copy-start.1
  1606.2 9.2 copy-start
  1606.2 547.8 %all-to-all-start.5 = ((bf16[64,4,128,384]{3,2,1,0:T(8,128)(2,1)}), bf16[64,4,128,384]{3,2,1,0:T(8,128)(2,1)}, u32[]{:S(2)}, u32[]{:S(2)}) async-start(bf16[64,4,128,384]{3,2,1,0:T(8,128)(2,1)} %bitcast.102), calls=%async_computation.5 | async-start | bytes 50331648 | tf_op jit(solution)/shard_map/all_to_all | solution.py:43
  2154.0 68.7 %all-to-all-start.8 = ((bf16[8,8,5,4096]{3,1,2,0:T(8,128)(2,1)}), bf16[8,8,5,4096]{3,1,2,0:T(8,128)(2,1)}, u32[]{:S(2)}, u32[]{:S(2)}) async-start(bf16[8,8,5,4096]{3,1,2,0:T(8,128)(2,1)} %copy.110), calls=%async_computation.9 | async-start | bytes 5242880 | tf_op jit(solution)/shard_map/all_to_all | solution.py:83
  2162.5 30.2 %slice-start = ((s8[25165824]{0:T(1024)(128)(4,1)}), s8[4194304]{0:T(1024)(128)(4,1)S(1)}, s32[]{:S(2)}) async-start(s8[25165824]{0:T(1024)(128)(4,1)} %bitcast.99), calls=%async_computation.14 | async-start | bytes 8388608
  2168.3 24.5 %slice-start.1 = ((s8[25165824]{0:T(1024)(128)(4,1)}), s8[4194304]{0:T(1024)(128)(4,1)S(1)}, s32[]{:S(2)}) async-start(s8[25165824]{0:T(1024)(128)(4,1)} %bitcast.99), calls=%async_computation.15 | async-start | bytes 8388608
  2168.3 24.5 %slice-start.2 = ((s8[25165824]{0:T(1024)(128)(4,1)}), s8[4194304]{0:T(1024)(128)(4,1)S(1)}, s32[]{:S(2)}) async-start(s8[25165824]{0:T(1024)(128)(4,1)} %bitcast.99), calls=%async_computation.16 | async-start | bytes 8388608
  2168.3 24.5 %slice-start.3 = ((s8[25165824]{0:T(1024)(128)(4,1)}), s8[4194304]{0:T(1024)(128)(4,1)S(1)}, s32[]{:S(2)}) async-start(s8[25165824]{0:T(1024)(128)(4,1)} %bitcast.99), calls=%async_computation.17 | async-start | bytes 8388608
  2168.3 24.5 %slice-start.4 = ((s8[25165824]{0:T(1024)(128)(4,1)}), s8[4194304]{0:T(1024)(128)(4,1)S(1)}, s32[]{:S(2)}) async-start(s8[25165824]{0:T(1024)(128)(4,1)} %bitcast.99), calls=%async_computation.18 | async-start | bytes 8388608
  2168.3 24.5 %slice-start.5 = ((s8[25165824]{0:T(1024)(128)(4,1)}), s8[4194304]{0:T(1024)(128)(4,1)S(1)}, s32[]{:S(2)}) async-start(s8[25165824]{0:T(1024)(128)(4,1)} %bitcast.99), calls=%async_computation.19 | async-start | bytes 8388608
  2222.7 64.3 %all-to-all-start.6 = ((bf16[8,8,5,4096]{3,1,2,0:T(8,128)(2,1)}), bf16[8,8,5,4096]{3,1,2,0:T(8,128)(2,1)S(1)}, u32[]{:S(2)}, u32[]{:S(2)}) async-start(bf16[8,8,5,4096]{3,1,2,0:T(8,128)(2,1)} %copy.103), calls=%async_computation.6 | async-start | bytes 5242880 | tf_op jit(solution)/shard_map/all_to_all | solution.py:83
  2228.6 94.0 %reduce-scatter.5.cloned.1.call-start = ((), (), s32[]{:S(2)}) async-start(), calls=%async_computation.13 | async-start | bytes 3276800 | tf_op jit(solution)/shard_map/reduce_scatter | solution.py:95
  2268.4 88.2 %reduce-scatter.3.cloned.1.call-start = ((), (), s32[]{:S(2)}) async-start(), calls=%async_computation.12 | async-start | bytes 3276800 | tf_op jit(solution)/shard_map/reduce_scatter | solution.py:95
  2322.5 42.0 %copy-start.2 = (f32[2,16,8]{1,2,0:T(8,128)S(1)}, f32[2,16,8]{1,2,0:T(8,128)}, u32[]{:S(2)}) copy-start(f32[2,16,8]{1,2,0:T(8,128)} %param.14) | copy-start | bytes 3076
  2322.5 42.1 %copy-start.6 = (s32[128]{0:T(128)S(1)}, s32[128]{0:T(128)}, u32[]{:S(2)}) copy-start(s32[128]{0:T(128)} %get-tuple-element.15) | copy-start | bytes 1540
  2322.5 42.1 %copy-start.5 = (s32[128]{0:T(128)S(1)}, s32[128]{0:T(128)}, u32[]{:S(2)}) copy-start(s32[128]{0:T(128)} %get-tuple-element.28) | copy-start | bytes 1540
  2324.9 34.0 %all-to-all-start.9 = ((bf16[8,8,5,1024]{3,1,2,0:T(8,128)(2,1)}), bf16[8,8,5,1024]{3,1,2,0:T(8,128)(2,1)S(1)}, u32[]{:S(2)}, u32[]{:S(2)}) async-start(bf16[8,8,5,1024]{3,1,2,0:T(8,128)(2,1)} %copy.113), calls=%async_computation.11 | async-start | bytes 1310720 | tf_op jit(solution)/shard_map/all_to_all | solution.py:101
  2358.8 25.2 %copy-start.4 = (pred[128]{0:T(512)(128)(4,1)S(1)}, pred[128]{0:T(512)(128)(4,1)}, u32[]{:S(2)}) copy-start(pred[128]{0:T(512)(128)(4,1)} %get-tuple-element.14) | copy-start | bytes 388
  2358.8 25.5 %copy-start.3 = (pred[128]{0:T(512)(128)(4,1)S(1)}, pred[128]{0:T(512)(128)(4,1)}, u32[]{:S(2)}) copy-start(pred[128]{0:T(512)(128)(4,1)} %get-tuple-element.27) | copy-start | bytes 388
  2358.9 22.8 all-to-all-start.7
Sparse Core Ops, SparseCore 0:
  2268.5 35.7 reduce-scatter.4
  2322.7 33.8 reduce-scatter.2
where the time goes:
time: 2400 us; the launch traced here: 2390 us
  blocking collectives  1100 us (46%)
  waiting for transfers between devices  938 us (39%)
  local copies, waits for them, and re-layouts  178 us (7%)
  matrix products  76.8 us (3%)
  other arithmetic  44.7 us (2%)
  starting transfers between devices  44.5 us (2%)
    all_to_all x1, blocking collectives, body(): lax.all_to_all(select_pieces(block_gate), 'ep', split_axis=0, concat_axis...  551 us
    all_to_all x1, blocking collectives, body(): lax.all_to_all(select_pieces(block_up), 'ep', split_axis=0, concat_axis=2...  544 us
    all_to_all x1, waiting for transfers between devices, body(): lax.all_to_all(select_pieces(block_down), 'ep', split_axis=0, concat_axis...  529 us
    all_to_all x1, waiting for transfers between devices, body(): lax.all_to_all(train_down, 'ep', split_axis=1, concat_axis=0, tiled=True)  129 us
    all_to_all x1, waiting for transfers between devices, body(): lax.all_to_all(train_up, 'ep', split_axis=1, concat_axis=0, tiled=True)  128 us
    all_to_all x1, waiting for transfers between devices, body(): lax.all_to_all(train_gate, 'ep', split_axis=1, concat_axis=0, tiled=True)  89.1 us
  transfers between devices with their start and end apart: 10, of which 7 were waited for; matrix products, arithmetic and copies ran while one was open for 9% of the time, Pallas kernels for 0%

commit v1 on v0

v1 whole, which is shorter than its diff:
```python
import functools

import jax
import jax.numpy as jnp
from jax import lax
from jax.experimental import pallas as pl
from jax.experimental.pallas import tpu as pltpu
from jax.sharding import PartitionSpec as P

EXPERTS = 16
MOST = 10
MESH = pl.DeviceIdType.MESH


def relay_kernel(
    pairs, chunk_rows, buffers, idx_ref, t0, t1, t2, o0, o1, o2, held, whole, own, other,
    local_sem, first_send, first_recv, line_send, line_recv,
    own_sem, other_send, other_recv, stage_sem, credit_x, credit_up, credit_down,
):
    trains, outs = (t0, t1, t2), (o0, o1, o2)
    me = lax.axis_index("ep")
    z, x = lax.div(me, 2), lax.rem(me, 2)
    partner = me + 1 - 2 * x
    above, below = me + 2, me - 2
    local = t0.shape[0]
    half = t0.shape[1] // 2
    steps = half // chunk_rows
    total = len(trains) * steps
    layer = 2 * local
    picks = own.shape[1]
    recv_slots = other_recv.shape[0]
    has_up, has_down = z < pairs - 1, z > 0

    barrier = pltpu.get_barrier_semaphore()
    pl.semaphore_signal(barrier, inc=1, device_id={"ep": partner}, device_id_type=MESH)

    @pl.when(has_up)
    def _():
        pl.semaphore_signal(barrier, inc=1, device_id={"ep": above}, device_id_type=MESH)

    @pl.when(has_down)
    def _():
        pl.semaphore_signal(barrier, inc=1, device_id={"ep": below}, device_id_type=MESH)

    pl.semaphore_wait(barrier, 1 + jnp.where(has_up, 1, 0) + jnp.where(has_down, 1, 0))

    def rows_of(side, step):
        return pl.ds(pl.multiple_of(side * half + step * chunk_rows, chunk_rows), chunk_rows)

    def mine(slot):
        return held.at[slot, pl.ds(me * local, local)]

    def region(slot, level):
        return held.at[slot, pl.ds(level * layer, layer)]

    def load_copy(train, step, slot):
        return pltpu.make_async_copy(
            train.at[:, rows_of(x, step), :], mine(slot), local_sem.at[slot]
        )

    def first_copy(train, step, slot):
        return pltpu.make_async_remote_copy(
            src_ref=train.at[:, rows_of(1 - x, step), :],
            dst_ref=mine(slot),
            send_sem=first_send.at[slot],
            recv_sem=first_recv.at[slot],
            device_id={"ep": partner},
            device_id_type=MESH,
        )

    def up_copy(slot, level):
        return pltpu.make_async_remote_copy(
            src_ref=region(slot, level),
            dst_ref=region(slot, level),
            send_sem=line_send.at[slot, level],
            recv_sem=line_recv.at[slot, level],
            device_id={"ep": above},
            device_id_type=MESH,
        )

    def down_copy(slot, level):
        return pltpu.make_async_remote_copy(
            src_ref=region(slot, level),
            dst_ref=region(slot, level),
            send_sem=line_send.at[slot, level + 1],
            recv_sem=line_recv.at[slot, level],
            device_id={"ep": below},
            device_id_type=MESH,
        )

    def own_copy(out, step, stage):
        return pltpu.make_async_copy(
            own.at[stage], out.at[:, rows_of(x, step), :], own_sem.at[stage]
        )

    def other_copy(out, step, stage, recv_slot):
        return pltpu.make_async_remote_copy(
            src_ref=other.at[stage],
            dst_ref=out.at[:, rows_of(x, step), :],
            send_sem=other_send.at[stage],
            recv_sem=other_recv.at[recv_slot],
            device_id={"ep": partner},
            device_id_type=MESH,
        )

    def stage_start(n):
        slot = lax.rem(n, buffers)

        @pl.when(n >= buffers)
        def _():
            pl.semaphore_wait(credit_x, 1)

        for a in range(len(trains)):

            @pl.when((n >= a * steps) & (n < (a + 1) * steps))
            def _():
                first_copy(trains[a], n - a * steps, slot).start()
                load_copy(trains[a], n - a * steps, slot).start()

    def stage_send(n):
        slot = lax.rem(n, buffers)
        load_copy(t0, 0, slot).wait()
        first_copy(t0, 0, slot).wait()

        @pl.when(has_up)
        def _():
            @pl.when(n >= buffers)
            def _():
                pl.semaphore_wait(credit_up, 1)

            up_copy(slot, z).start()

        @pl.when(has_down)
        def _():
            @pl.when(n >= buffers)
            def _():
                pl.semaphore_wait(credit_down, 1)

            down_copy(slot, z).start()

    def stage_forward(n, distance):
        slot = lax.rem(n, buffers)

        @pl.when(z - distance >= 0)
        def _():
            up_copy(slot, z - distance).wait_recv()

            @pl.when(has_up)
            def _():
                up_copy(slot, z - distance).start()

        @pl.when(z + distance < pairs)
        def _():
            down_copy(slot, z + distance).wait_recv()

            @pl.when(has_down)
            def _():
                down_copy(slot, z + distance).start()

    def stage_finish(n):
        slot = lax.rem(n, buffers)
        stage = lax.rem(n, 2)
        taken = pltpu.make_async_copy(held.at[slot], whole, stage_sem)
        taken.start()

        def drain_up(level, carry):
            up_copy(slot, level).wait_send()
            return carry

        def drain_down(level, carry):
            down_copy(slot, level).wait_send()
            return carry

        @pl.when(has_up)
        def _():
            lax.fori_loop(0, z + 1, drain_up, 0)

        @pl.when(has_down)
        def _():
            lax.fori_loop(z, pairs, drain_down, 0)

        taken.wait()

        @pl.when(n < total - buffers)
        def _():
            pl.semaphore_signal(credit_x, inc=1, device_id={"ep": partner}, device_id_type=MESH)

            @pl.when(has_up)
            def _():
                pl.semaphore_signal(
                    credit_down, inc=1, device_id={"ep": above}, device_id_type=MESH
                )

            @pl.when(has_down)
            def _():
                pl.semaphore_signal(
                    credit_up, inc=1, device_id={"ep": below}, device_id_type=MESH
                )

        @pl.when(n >= 2)
        def _():
            own_copy(o0, 0, stage).wait()
            other_copy(o0, 0, stage, 0).wait_send()

        @pl.when(n >= 1)
        def _():
            other_copy(o0, 0, stage, lax.rem(n - 1, recv_slots)).wait_recv()

        def pick(s, carry):
            other[stage, s] = whole[idx_ref[picks + s]]
            own[stage, s] = whole[idx_ref[s]]
            return carry

        lax.fori_loop(0, picks, pick, 0)
        for a in range(len(trains)):

            @pl.when((n >= a * steps) & (n < (a + 1) * steps))
            def _():
                other_copy(outs[a], n - a * steps, stage, lax.rem(n, recv_slots)).start()
                own_copy(outs[a], n - a * steps, stage).start()

    def iteration(i, carry):
        @pl.when(i < total)
        def _():
            stage_start(i)

        @pl.when((i >= 1) & (i - 1 < total))
        def _():
            stage_send(i - 1)

        def hop(distance, inner):
            n = i - 1 - distance

            @pl.when((n >= 0) & (n < total))
            def _():
                stage_forward(n, distance)

            return inner

        lax.fori_loop(1, pairs, hop, 0)

        @pl.when(i >= pairs)
        def _():
            stage_finish(i - pairs)

        return carry

    lax.fori_loop(0, total + pairs, iteration, 0)
    for n in range(max(total - 2, 0), total):
        own_copy(o0, 0, n % 2).wait()
        other_copy(o0, 0, n % 2, 0).wait_send()
    other_copy(o0, 0, 0, (total - 1) % recv_slots).wait_recv()


def relay(idx, trains, ep_count, part_count):
    local, piece_rows, width = trains[0].shape
    pairs = ep_count // 2
    slots = ep_count * local
    buffers = pairs + 3
    chunk_rows = 32
    while chunk_rows > 16 and buffers * slots * chunk_rows * width * 2 > 24 * 2**20:
        chunk_rows //= 2
    picks = local * part_count
    dma = pltpu.SemaphoreType.DMA
    any_spec = pl.BlockSpec(memory_space=pl.ANY)
    return pl.pallas_call(
        functools.partial(relay_kernel, pairs, chunk_rows, buffers),
        out_shape=[jax.ShapeDtypeStruct((picks, piece_rows, width), jnp.bfloat16)] * 3,
        in_specs=[pl.BlockSpec(memory_space=pltpu.SMEM)] + [any_spec] * 3,
        out_specs=[any_spec] * 3,
        scratch_shapes=[
            pltpu.VMEM((buffers, slots, chunk_rows, width), jnp.bfloat16),
            pltpu.VMEM((slots, chunk_rows, width), jnp.bfloat16),
            pltpu.VMEM((2, picks, chunk_rows, width), jnp.bfloat16),
            pltpu.VMEM((2, picks, chunk_rows, width), jnp.bfloat16),
            dma((buffers,)),
            dma((buffers,)),
            dma((buffers,)),
            dma((buffers, pairs + 1)),
            dma((buffers, pairs)),
            dma((2,)),
            dma((2,)),
            dma((buffers + 2,)),
            dma,
            pltpu.SemaphoreType.REGULAR,
            pltpu.SemaphoreType.REGULAR,
            pltpu.SemaphoreType.REGULAR,
        ],
        compiler_params=pltpu.CompilerParams(
            collective_id=0, has_side_effects=True, vmem_limit_bytes=56 * 2**20
        ),
    )(idx, *trains)


def body(
    tokens, route_ids, route_weights, train_map, serve_place, train_gate, train_up, train_down
):
    ep_count = lax.axis_size("ep")
    tp_count = lax.axis_size("tp")
    ep_index = lax.axis_index("ep")
    slot_count = serve_place.shape[0]
    local_slots, piece_rows, quarter_width = train_gate.shape
    part_count = slot_count // EXPERTS
    slot_iota = jnp.arange(slot_count, dtype=jnp.int32)
    inverse = jnp.sum(
        jnp.where(train_map[:, None] == slot_iota[None, :], slot_iota[:, None], 0), axis=0
    )
    wanted = (
        serve_place[:, None] * part_count + jnp.arange(part_count, dtype=jnp.int32)[None, :]
    ).reshape(-1)
    source_slot = jnp.sum(
        jnp.where(wanted[:, None] == slot_iota[None, :], inverse[None, :], 0), axis=1
    ).reshape(ep_count, local_slots * part_count)
    partner = ep_index + 1 - 2 * (ep_index % 2)
    idx = jnp.concatenate(
        [
            lax.dynamic_index_in_dim(source_slot, ep_index, 0, keepdims=False),
            lax.dynamic_index_in_dim(source_slot, partner, 0, keepdims=False),
        ]
    ).astype(jnp.int32)
    model_rows = part_count * piece_rows
    serve_gate, serve_up, serve_down = (
        o.reshape(local_slots, model_rows, quarter_width)
        for o in relay(idx, (train_gate, train_up, train_down), ep_count, part_count)
    )

    step_count, tok_count, model_width = tokens.shape
    topk_count = route_ids.shape[2]
    pair_count = tok_count * topk_count
    capacity = (MOST + 1) // 2
    buffer_rows = slot_count * capacity
    out_width = model_width // tp_count
    same_slot = serve_place[:, None] == serve_place[None, :]
    replica_rank = jnp.sum(same_slot & (slot_iota[None, :] < slot_iota[:, None]), axis=1)
    pair_iota = jnp.arange(pair_count, dtype=jnp.int32)

    def place(ids):
        pair_experts = ids.reshape(pair_count)
        holders = serve_place[None, :] == pair_experts[:, None]
        replica_count = jnp.sum(holders, axis=1)
        earlier_pairs = (pair_experts[:, None] == pair_experts[None, :]) & (
            pair_iota[None, :] < pair_iota[:, None]
        )
        seen = jnp.sum(earlier_pairs, axis=1)
        target = (seen + ep_index) % replica_count
        position = seen // replica_count
        chosen = holders & (replica_rank[None, :] == target[:, None])
        dest_slot = jnp.sum(jnp.where(chosen, slot_iota[None, :], 0), axis=1)
        row_index = dest_slot * capacity + position
        placing = row_index[None, :] == jnp.arange(buffer_rows, dtype=jnp.int32)[:, None]
        return placing.reshape(buffer_rows, tok_count, topk_count)

    placing = jax.vmap(place)(route_ids)
    send_rows = jnp.einsum(
        "tbi,tid->btd",
        jnp.any(placing, axis=3).astype(jnp.bfloat16),
        tokens,
        preferred_element_type=jnp.float32,
    ).astype(jnp.bfloat16)
    send_rows = send_rows.reshape(ep_count, local_slots, capacity * step_count, model_width)
    received = lax.all_to_all(send_rows, "ep", split_axis=0, concat_axis=0, tiled=True)
    received = received.transpose(1, 0, 2, 3).reshape(
        local_slots, ep_count * capacity * step_count, model_width
    )
    gate_act = jnp.einsum("lmd,ldf->lmf", received, serve_gate, preferred_element_type=jnp.float32)
    up_act = jnp.einsum("lmd,ldf->lmf", received, serve_up, preferred_element_type=jnp.float32)
    hidden = (jax.nn.silu(gate_act) * up_act).astype(jnp.bfloat16)
    partial_value = jnp.einsum(
        "lmf,ldf->lmd", hidden, serve_down, preferred_element_type=jnp.float32
    ).astype(jnp.bfloat16)
    partial_value = lax.optimization_barrier(partial_value)
    summed = lax.psum_scatter(partial_value, "tp", scatter_dimension=2, tiled=True)
    summed = summed.reshape(
        local_slots, ep_count, capacity * step_count, out_width
    ).transpose(1, 0, 2, 3)
    returned = lax.all_to_all(summed, "ep", split_axis=0, concat_axis=0, tiled=True)
    flat_out = returned.reshape(buffer_rows, step_count, out_width)
    mixing = jnp.sum(jnp.where(placing, route_weights[:, None], 0.0), axis=3)
    moe_out = jnp.einsum(
        "tbi,btd->tid",
        mixing,
        flat_out.astype(jnp.float32),
        precision=lax.Precision.HIGHEST,
        preferred_element_type=jnp.float32,
    ).astype(jnp.bfloat16)
    return (serve_gate, serve_up, serve_down, moe_out)


def solution(mesh):
    in_specs = (
        P(None, "ep", None),
        P(None, "ep", None),
        P(None, "ep", None),
        P(),
        P(),
        P("ep", None, "tp"),
        P("ep", None, "tp"),
        P("ep", None, "tp"),
    )
    out_specs = (P("ep", None, "tp"), P("ep", None, "tp"), P("ep", None, "tp"), P(None, "ep", "tp"))
    return jax.shard_map(body, mesh=mesh, in_specs=in_specs, out_specs=out_specs, check_vma=False)
```

time: 2400 us -> 1610 us (0.67)
  Pallas kernels: 0 us -> 1350 us
  blocking collectives: 1100 us -> 0 us
  waiting for transfers between devices: 938 us -> 84.2 us
  local copies, waits for them, and re-layouts: 178 us -> 95.7 us
  other arithmetic: 44.7 us -> 4.14 us
  starting transfers between devices: 44.5 us -> 13 us
  matrix products: 76.8 us -> 50.6 us
    pallas_call x0 -> x1, Pallas kernels: none -> 1350 us  [relay(): pl.pallas_call(functools.partial(relay_kernel, pairs, chunk_rows, buffers...]
    all_to_all x2 -> x0, blocking collectives: 1100 us -> none  [the longest x1 551 us: body(): lax.all_to_all(select_pieces(block_gate), 'ep', split_axis=0, concat_axis...]
    all_to_all x4 -> x0, waiting for transfers between devices: 876 us -> none  [the longest x1 529 us: body(): lax.all_to_all(select_pieces(block_down), 'ep', split_axis=0, concat_axis...]
    all_to_all x6 -> x0, local copies, waits for them, and re-layouts: 75 us -> none  [the longest x1 24.4 us: body(): lax.all_to_all(select_pieces(block_gate), 'ep', split_axis=0, concat_axis...]
    gather x6 -> x0, local copies, waits for them, and re-layouts: 51.6 us -> none  [the longest x3 48 us: select_pieces(): jnp.take(blocks, source_slot, axis=0)]
    select_n x4 -> x0, other arithmetic: 41.5 us -> none  [the longest x1 41.3 us: select_pieces(): jnp.take(blocks, source_slot, axis=0)]
    unnamed x33 -> x27, local copies, waits for them, and re-layouts: 27.6 us -> 54.8 us
    dot_general x8 -> x4, matrix products: 76.8 us -> 50.6 us  [the longest x1 26.1 us: body(): jnp.einsum('lmf,ldf->lmd', hidden, serve_down, preferred_element_type=jnp...]
  transfers between devices with their start and end apart: 10 -> 3, of which waited for: 7 -> 2; matrix products, arithmetic and copies ran while one was open for 9% -> 0% of each run, Pallas kernels for 0% -> 84%
where the time goes in v1:
time: 1610 us
  Pallas kernels  1350 us (84%)
  local copies, waits for them, and re-layouts  95.7 us (6%)
  waiting for transfers between devices  84.2 us (5%)
  matrix products  50.6 us (3%)
    pallas_call x1, Pallas kernels, relay(): pl.pallas_call(functools.partial(relay_kernel, pairs, chunk_rows, buffers...  1350 us
    unnamed x27, local copies, waits for them, and re-layouts  54.8 us
    reduce_scatter x1, waiting for transfers between devices, body(): lax.psum_scatter(partial_value, 'tp', scatter_dimension=2, tiled=True)  53.1 us
  transfers between devices with their start and end apart: 3, of which 2 were waited for; matrix products, arithmetic and copies ran while one was open for 0% of the time, Pallas kernels for 84%

profile of v1, /device:TPU:0, one launch (start us, length us, event | category | flops | bytes accessed | tf_op | source)
XLA Modules:
  0.0 1608.6 jit_solution(657963677701749777)
XLA Ops:
  7.2 0.8 copy.30
  8.1 0.9 convert_reduce_fusion.1
  9.0 0.8 fusion.25
  9.8 0.2 convert_reduce_fusion
  10.0 0.1 compare_and_fusion.1
  10.1 0.1 fusion.29
  10.2 0.8 select_reduce_fusion.1
  11.2 0.1 and.46
  11.3 0.2 fusion.24
  11.5 3.9 fusion
  15.4 10.3 copy.32
  25.8 13.7 reshape.124
  39.5 9.1 copy.33
  48.6 7.4 all-to-all-start
  56.1 0.1 add.73
  56.2 0.1 select_reduce_fusion.3
  56.3 0.1 select_reduce_fusion.2
  56.5 0.6 pad_add_fusion.idx_ref
  57.1 1346.8 %shard_map.111 = (bf16[32,1024,384]{2,1,0:T(8,128)(2,1)}, bf16[32,1024,384]{2,1,0:T(8,128)(2,1)}, bf16[32,1024,384]{2,1,0:T(8,128)(2,1)}) custom-call(s32[64]{0:T(128)} %pad_add_fusion.idx_ref, bf16[8,1024,384]{2,1,0:T(8,128)(2,1)} %t0.1, bf16[8,1024,384]{2,1,0:T(8,128)(2,1)} %t1.1, bf16[8,1024,384]{2,1,0:T(8,128)(2,1)} %t2.1), custom_call_target="tpu_custom_call" | custom-call | tf_op jit(solution)/shard_map/pallas_call | solution.py:266
  1404.0 17.7 %fusion.3 = f32[8,80,384]{2,1,0:T(8,128)S(1)} fusion(bf16[8,4096,384]{2,1,0:T(8,128)(2,1)} %bitcast.21, bf16[8,80,4096]{2,0,1:T(8,128)(2,1)} %bitcast.7), kind=kOutput, calls=%fused_computation.5 | convolution fusion | flops 2013265920 | bytes 31391744 | tf_op jit(solution)/shard_map/lmd,ldf->lmf/dot_general | solution.py:365
  1421.7 26.1 %convolution_convert_fusion = bf16[8,80,4096]{2,1,0:T(8,128)(2,1)} fusion(bf16[8,4096,384]{2,1,0:T(8,128)(2,1)} %bitcast.23, bf16[8,4096,384]{2,1,0:T(8,128)(2,1)} %bitcast.27, bf16[8,80,4096]{2,0,1:T(8,128)(2,1)} %bitcast.7, f32[8,80,384]{2,1,0:T(8,128)S(1)} %fusion.3), kind=kOutput, calls=%fused_computation | convolution fusion | flops 4030627840 | bytes 61800448 | tf_op jit(solution)/shard_map/lmf,ldf->lmd/dot_general | solution.py:368
  1447.8 53.1 %reduce-scatter.2.cloned.1.call-done = bf16[8,80,1024]{2,1,0:T(8,128)(2,1)} async-done(((bf16[8,80,4096]{2,1,0:T(8,128)(2,1)}), bf16[8,80,1024]{2,1,0:T(8,128)(2,1)}) %reduce-scatter.2.cloned.1.call-update) | async-done | bytes 1310736 | tf_op jit(solution)/shard_map/reduce_scatter | solution.py:372
  1500.9 3.1 copy.36
  1504.0 5.5 all-to-all-start.1
  1509.6 0.2 select_reduce_fusion
  1509.8 31.0 %all-to-all-done.1 = bf16[8,8,10,1024]{3,1,2,0:T(8,128)(2,1)} async-done(((bf16[8,8,10,1024]{3,1,2,0:T(8,128)(2,1)}), bf16[8,8,10,1024]{3,1,2,0:T(8,128)(2,1)}, u32[]{:S(2)}, u32[]{:S(2)}) %all-to-all-start.1) | async-done | bytes 1310752 | tf_op jit(solution)/shard_map/all_to_all | solution.py:376
  1540.8 2.2 copy.37
  1543.0 1.9 reshape.127
  1544.9 2.9 fusion.15
  1547.8 22.5 %copy.56 = bf16[8,4096,384]{2,1,0:T(8,128)(2,1)} copy(bf16[8,4096,384]{2,1,0:T(8,128)(2,1)} %bitcast.22) | data formatting | bytes 50331648
  1570.3 22.5 %copy.57 = bf16[8,4096,384]{2,1,0:T(8,128)(2,1)} copy(bf16[8,4096,384]{2,1,0:T(8,128)(2,1)} %bitcast.28) | data formatting | bytes 50331648
  1592.9 8.9 copy.58
  (37 shorter events, 0.6 us)
Async XLA Ops:
  7.2 4.3 copy-start
  48.5 7.5 copy-start.3
  48.5 7.7 copy-start.4
  48.6 1355.4 %all-to-all-start = ((bf16[8,8,10,4096]{3,1,2,0:T(8,128)(2,1)}), bf16[8,8,10,4096]{3,1,2,0:T(8,128)(2,1)}, u32[]{:S(2)}, u32[]{:S(2)}) async-start(bf16[8,8,10,4096]{3,1,2,0:T(8,128)(2,1)} %copy.33), calls=%async_computation | async-start | bytes 10485760 | tf_op jit(solution)/shard_map/all_to_all | solution.py:361
  56.0 1444.9 %reduce-scatter.2.cloned.1.call-start = ((), (), s32[]{:S(2)}) async-start(), calls=%async_computation.3 | async-start | bytes 6553600 | tf_op jit(solution)/shard_map/reduce_scatter | solution.py:372
  1447.8 61.8 %copy-start.2 = (f32[2,16,8]{1,2,0:T(8,128)S(1)}, f32[2,16,8]{1,2,0:T(8,128)}, u32[]{:S(2)}) copy-start(f32[2,16,8]{1,2,0:T(8,128)} %param.10) | copy-start | bytes 3076
  1504.0 36.8 %all-to-all-start.1 = ((bf16[8,8,10,1024]{3,1,2,0:T(8,128)(2,1)}), bf16[8,8,10,1024]{3,1,2,0:T(8,128)(2,1)}, u32[]{:S(2)}, u32[]{:S(2)}) async-start(bf16[8,8,10,1024]{3,1,2,0:T(8,128)(2,1)} %bitcast.10), calls=%async_computation.2 | async-start | bytes 2621440 | tf_op jit(solution)/shard_map/all_to_all | solution.py:376
  1547.8 45.0 %slice-start = ((s8[25165824]{0:T(1024)(128)(4,1)}), s8[4194304]{0:T(1024)(128)(4,1)S(1)}, s32[]{:S(2)}) async-start(s8[25165824]{0:T(1024)(128)(4,1)} %bitcast.24), calls=%async_computation.4 | async-start | bytes 8388608
  1547.8 45.0 %slice-start.1 = ((s8[25165824]{0:T(1024)(128)(4,1)}), s8[4194304]{0:T(1024)(128)(4,1)S(1)}, s32[]{:S(2)}) async-start(s8[25165824]{0:T(1024)(128)(4,1)} %bitcast.24), calls=%async_computation.5 | async-start | bytes 8388608
  1547.8 45.0 %slice-start.2 = ((s8[25165824]{0:T(1024)(128)(4,1)}), s8[4194304]{0:T(1024)(128)(4,1)S(1)}, s32[]{:S(2)}) async-start(s8[25165824]{0:T(1024)(128)(4,1)} %bitcast.24), calls=%async_computation.6 | async-start | bytes 8388608
  1570.3 22.5 %slice-start.3 = ((s8[25165824]{0:T(1024)(128)(4,1)}), s8[4194304]{0:T(1024)(128)(4,1)S(1)}, s32[]{:S(2)}) async-start(s8[25165824]{0:T(1024)(128)(4,1)} %bitcast.24), calls=%async_computation.7 | async-start | bytes 8388608
  1570.3 22.5 %slice-start.4 = ((s8[25165824]{0:T(1024)(128)(4,1)}), s8[4194304]{0:T(1024)(128)(4,1)S(1)}, s32[]{:S(2)}) async-start(s8[25165824]{0:T(1024)(128)(4,1)} %bitcast.24), calls=%async_computation.8 | async-start | bytes 8388608
  1570.3 22.5 %slice-start.5 = ((s8[25165824]{0:T(1024)(128)(4,1)}), s8[4194304]{0:T(1024)(128)(4,1)S(1)}, s32[]{:S(2)}) async-start(s8[25165824]{0:T(1024)(128)(4,1)} %bitcast.24), calls=%async_computation.9 | async-start | bytes 8388608
  1592.8 8.9 copy-start.1
Sparse Core Ops, SparseCore 0:
  1447.9 52.9 reduce-scatter.1

commit v2 on v1

--- a/solution.py
+++ b/solution.py
@@ -319,22 +319,23 @@
         ]
     ).astype(jnp.int32)
     model_rows = part_count * piece_rows
-    serve_gate, serve_up, serve_down = (
+    raw_gate, raw_up, raw_down = (
         o.reshape(local_slots, model_rows, quarter_width)
         for o in relay(idx, (train_gate, train_up, train_down), ep_count, part_count)
     )
 
     step_count, tok_count, model_width = tokens.shape
     topk_count = route_ids.shape[2]
-    pair_count = tok_count * topk_count
     capacity = (MOST + 1) // 2
-    buffer_rows = slot_count * capacity
-    out_width = model_width // tp_count
+    depth = capacity * step_count
+    peer_rows = depth * local_slots
+    all_tokens = step_count * tok_count
     same_slot = serve_place[:, None] == serve_place[None, :]
     replica_rank = jnp.sum(same_slot & (slot_iota[None, :] < slot_iota[:, None]), axis=1)
+    pair_count = tok_count * topk_count
     pair_iota = jnp.arange(pair_count, dtype=jnp.int32)
 
-    def place(ids):
+    def rows(ids, decode_step):
         pair_experts = ids.reshape(pair_count)
         holders = serve_place[None, :] == pair_experts[:, None]
         replica_count = jnp.sum(holders, axis=1)
@@ -346,44 +347,77 @@
         position = seen // replica_count
         chosen = holders & (replica_rank[None, :] == target[:, None])
         dest_slot = jnp.sum(jnp.where(chosen, slot_iota[None, :], 0), axis=1)
-        row_index = dest_slot * capacity + position
-        placing = row_index[None, :] == jnp.arange(buffer_rows, dtype=jnp.int32)[:, None]
-        return placing.reshape(buffer_rows, tok_count, topk_count)
-
-    placing = jax.vmap(place)(route_ids)
-    send_rows = jnp.einsum(
-        "tbi,tid->btd",
-        jnp.any(placing, axis=3).astype(jnp.bfloat16),
-        tokens,
+        return (
+            dest_slot // local_slots * peer_rows
+            + (decode_step * capacity + position) * local_slots
+            + dest_slot % local_slots
+        )
+
+    row_index = jax.vmap(rows)(route_ids, jnp.arange(step_count, dtype=jnp.int32))
+    row_index = row_index.reshape(1, all_tokens, topk_count)
+    buffer_iota = jnp.arange(ep_count * peer_rows, dtype=jnp.int32)
+    placing = row_index == buffer_iota[:, None, None]
+    mixing = jnp.sum(
+        jnp.where(placing, route_weights.reshape(1, all_tokens, topk_count), 0.0), axis=2
+    )
+    send_rows = jnp.dot(
+        jnp.any(placing, axis=2).astype(jnp.bfloat16),
+        tokens.reshape(all_tokens, model_width),
         preferred_element_type=jnp.float32,
     ).astype(jnp.bfloat16)
-    send_rows = send_rows.reshape(ep_count, local_slots, capacity * step_count, model_width)
-    received = lax.all_to_all(send_rows, "ep", split_axis=0, concat_axis=0, tiled=True)
-    received = received.transpose(1, 0, 2, 3).reshape(
-        local_slots, ep_count * capacity * step_count, model_width
-    )
-    gate_act = jnp.einsum("lmd,ldf->lmf", received, serve_gate, preferred_element_type=jnp.float32)
-    up_act = jnp.einsum("lmd,ldf->lmf", received, serve_up, preferred_element_type=jnp.float32)
+    received = lax.all_to_all(
+        send_rows.reshape(ep_count, depth, local_slots, model_width),
+        "ep", split_axis=0, concat_axis=0, tiled=True,
+    ).reshape(ep_count * depth, local_slots, model_width)
+    mix = lax.all_to_all(
+        mixing.reshape(ep_count, peer_rows, all_tokens),
+        "ep", split_axis=0, concat_axis=0, tiled=True,
+    )
+    gate_act = jnp.einsum("mld,ldf->lmf", received, raw_gate, preferred_element_type=jnp.float32)
+    up_act = jnp.einsum("mld,ldf->lmf", received, raw_up, preferred_element_type=jnp.float32)
     hidden = (jax.nn.silu(gate_act) * up_act).astype(jnp.bfloat16)
     partial_value = jnp.einsum(
-        "lmf,ldf->lmd", hidden, serve_down, preferred_element_type=jnp.float32
+        "lmf,ldf->lmd", hidden, raw_down, preferred_element_type=jnp.float32
     ).astype(jnp.bfloat16)
-    partial_value = lax.optimization_barrier(partial_value)
-    summed = lax.psum_scatter(partial_value, "tp", scatter_dimension=2, tiled=True)
-    summed = summed.reshape(
-        local_slots, ep_count, capacity * step_count, out_width
-    ).transpose(1, 0, 2, 3)
+    mix = mix.reshape(ep_count, depth, local_slots, all_tokens)
+    mix_high = mix.astype(jnp.bfloat16)
+    mix_low = (mix - mix_high.astype(jnp.float32)).astype(jnp.bfloat16)
+    rows_out = partial_value.reshape(local_slots, ep_count, depth, model_width)
+
+    def combine(part):
+        return jnp.einsum("pclt,lpcd->ptd", part, rows_out, preferred_element_type=jnp.float32)
+
+    combined = (combine(mix_high) + combine(mix_low)).astype(jnp.bfloat16)
+    combined = lax.optimization_barrier(combined)
+    summed = lax.psum_scatter(combined, "tp", scatter_dimension=2, tiled=True)
+    raw_gate, raw_up, raw_down, _ = lax.optimization_barrier(
+        (raw_gate, raw_up, raw_down, combined)
+    )
+    serve_gate, serve_up, serve_down = (settle(o) for o in (raw_gate, raw_up, raw_down))
+    summed, serve_gate, serve_up = lax.optimization_barrier((summed, serve_gate, serve_up))
     returned = lax.all_to_all(summed, "ep", split_axis=0, concat_axis=0, tiled=True)
-    flat_out = returned.reshape(buffer_rows, step_count, out_width)
-    mixing = jnp.sum(jnp.where(placing, route_weights[:, None], 0.0), axis=3)
-    moe_out = jnp.einsum(
-        "tbi,btd->tid",
-        mixing,
-        flat_out.astype(jnp.float32),
-        precision=lax.Precision.HIGHEST,
-        preferred_element_type=jnp.float32,
-    ).astype(jnp.bfloat16)
+    moe_out = jnp.sum(returned.astype(jnp.float32), axis=0).astype(jnp.bfloat16)
+    moe_out = moe_out.reshape(step_count, tok_count, model_width // tp_count)
     return (serve_gate, serve_up, serve_down, moe_out)
+
+
+def settle_kernel(source, target):
+    target[...] = source[...]
+
+
+def settle(source):
+    slots, rows, width = source.shape
+    spec = pl.BlockSpec((1, rows, width), lambda i: (i, 0, 0))
+    return pl.pallas_call(
+        settle_kernel,
+        grid=(slots,),
+        out_shape=jax.ShapeDtypeStruct(source.shape, source.dtype),
+        in_specs=[spec],
+        out_specs=spec,
+        cost_estimate=pl.CostEstimate(
+            flops=0, bytes_accessed=4 * slots * rows * width, transcendentals=0
+        ),
+    )(source)
 
 
 def solution(mesh):

time: 1610 us -> 1510 us (0.938)
  local copies, waits for them, and re-layouts: 95.7 us -> 8.59 us
  waiting for transfers between devices: 84.2 us -> 3.15 us
  Pallas kernels: 1350 us -> 1400 us
    pallas_call x0 -> x3, Pallas kernels: none -> 55.9 us  [settle(): pl.pallas_call(settle_kernel, grid=(slots,), out_shape=jax.ShapeDtypeStru...]
    unnamed x27 -> x9, local copies, waits for them, and re-layouts: 54.8 us -> 0.83 us
    reduce_scatter x1, waiting for transfers between devices: 53.1 us -> 0.01 us  [body(): summed = lax.psum_scatter(combined, 'tp', scatter_dimension=2, tiled=True)]
    all_to_all x1, waiting for transfers between devices: 31 us -> 0.01 us  [body(): lax.all_to_all(summed, 'ep', split_axis=0, concat_axis=0, tiled=True)]
    reshape x3 -> x2, local copies, waits for them, and re-layouts: 24.7 us -> 0.78 us  [body(): mixing.reshape(ep_count, peer_rows, all_tokens)]
    dot_general x4 -> x5, matrix products: 50.6 us -> 56.4 us  [the longest x1 26 us: body(): jnp.einsum('lmf,ldf->lmd', hidden, raw_down, preferred_element_type=jnp.f...]
  transfers between devices with their start and end apart: 3 -> 4, of which waited for: 2 -> 1; matrix products, arithmetic and copies ran while one was open for 0% -> 0% of each run, Pallas kernels for 84% -> 93%
where the time goes in v2:
time: 1510 us
  Pallas kernels  1400 us (93%)
  matrix products  56.4 us (4%)
  starting transfers between devices  18.6 us (1%)
    pallas_call x1, Pallas kernels, relay(): pl.pallas_call(functools.partial(relay_kernel, pairs, chunk_rows, buffers...  1350 us
    pallas_call x3, Pallas kernels, settle(): pl.pallas_call(settle_kernel, grid=(slots,), out_shape=jax.ShapeDtypeStru...  55.9 us
  transfers between devices with their start and end apart: 4, of which 1 were waited for; matrix products, arithmetic and copies ran while one was open for 0% of the time, Pallas kernels for 93%

profile of v2, /device:TPU:0, one launch (start us, length us, event | category | flops | bytes accessed | tf_op | source)
XLA Modules:
  0.0 1507.4 jit_solution(18290863376358785366)
XLA Ops:
  7.2 0.8 copy.47
  8.1 0.9 convert_reduce_fusion.1
  9.0 0.8 fusion.37
  9.8 0.2 convert_reduce_fusion
  10.0 0.1 compare_and_fusion.1
  10.2 0.1 and_select_fusion
  10.4 0.8 select_reduce_fusion.2
  11.4 0.8 copy.61
  12.3 0.3 select_reduce_fusion
  12.6 0.1 reshape.206
  12.7 0.7 copy.50
  13.4 7.3 all-to-all-start
  20.6 0.3 fusion.33
  20.9 3.9 convolution_convert_fusion.1
  24.8 3.1 all-to-all-done
  28.0 4.8 all-to-all-start.1
  33.0 0.1 add.124
  33.1 0.1 select_reduce_fusion.3
  33.2 0.1 select_reduce_fusion.1
  33.4 0.6 pad_add_fusion.idx_ref
  34.0 1345.5 %shard_map.111 = (bf16[32,1024,384]{2,1,0:T(8,128)(2,1)}, bf16[32,1024,384]{2,1,0:T(8,128)(2,1)}, bf16[32,1024,384]{2,1,0:T(8,128)(2,1)}) custom-call(s32[64]{0:T(128)} %pad_add_fusion.idx_ref, bf16[8,1024,384]{2,1,0:T(8,128)(2,1)} %t0.1, bf16[8,1024,384]{2,1,0:T(8,128)(2,1)} %t1.1, bf16[8,1024,384]{2,1,0:T(8,128)(2,1)} %t2.1), custom_call_target="tpu_custom_call" | custom-call | tf_op jit(solution)/shard_map/pallas_call | solution.py:266
  1379.5 0.1 copy.51
  1379.7 17.7 %fusion.18 = f32[8,80,384]{2,1,0:T(8,128)S(1)} fusion(bf16[8,4096,384]{2,1,0:T(8,128)(2,1)} %bitcast.34, bf16[80,8,4096]{2,1,0:T(8,128)(2,1)} %bitcast.4), kind=kOutput, calls=%fused_computation.12 | convolution fusion | flops 2013265920 | bytes 31391744 | tf_op jit(solution)/shard_map/mld,ldf->lmf/dot_general | solution.py:376
  1397.4 26.0 %convolution_convert_fusion = bf16[8,80,4096]{2,1,0:T(8,128)(2,1)} fusion(bf16[8,4096,384]{2,1,0:T(8,128)(2,1)} %bitcast.36, bf16[8,4096,384]{2,1,0:T(8,128)(2,1)} %bitcast.38, bf16[80,8,4096]{2,1,0:T(8,128)(2,1)} %bitcast.4, f32[8,80,384]{2,1,0:T(8,128)S(1)} %fusion.18), kind=kOutput, calls=%fused_computation.4 | convolution fusion | flops 4030627840 | bytes 61800448 | tf_op jit(solution)/shard_map/lmf,ldf->lmd/dot_general | solution.py:379
  1423.4 5.4 copy.55
  1428.7 3.6 fusion.4
  1432.4 5.1 fusion.13
  1437.5 18.8 %shard_map.112 = bf16[8,4096,384]{2,1,0:T(8,128)(2,1)} custom-call(bf16[8,4096,384]{2,1,0:T(8,128)(2,1)} %bitcast.35), custom_call_target="tpu_custom_call" | custom-call | bytes 50331648 | tf_op jit(solution)/shard_map/pallas_call | solution.py:411
  1456.3 18.6 %shard_map.113 = bf16[8,4096,384]{2,1,0:T(8,128)(2,1)} custom-call(bf16[8,4096,384]{2,1,0:T(8,128)(2,1)} %bitcast.39), custom_call_target="tpu_custom_call" | custom-call | bytes 50331648 | tf_op jit(solution)/shard_map/pallas_call | solution.py:411
  1474.8 6.5 all-to-all-start.2
  1481.3 18.6 %shard_map.114 = bf16[8,4096,384]{2,1,0:T(8,128)(2,1)} custom-call(bf16[8,4096,384]{2,1,0:T(8,128)(2,1)} %bitcast.37), custom_call_target="tpu_custom_call" | custom-call | bytes 50331648 | tf_op jit(solution)/shard_map/pallas_call | solution.py:411
  1499.9 0.7 reduce_sum.85
  (26 shorter events, 0.8 us)
Async XLA Ops:
  7.2 13.7 copy-start
  13.4 14.6 all-to-all-start
  28.0 4.9 copy-start.2
  28.0 5.1 copy-start.3
  28.0 1351.7 %all-to-all-start.1 = ((bf16[8,10,8,4096]{3,2,1,0:T(8,128)(2,1)}), bf16[8,10,8,4096]{3,2,1,0:T(8,128)(2,1)}, u32[]{:S(2)}, u32[]{:S(2)}) async-start(bf16[8,10,8,4096]{3,2,1,0:T(8,128)(2,1)} %bitcast.40), calls=%async_computation.1 | async-start | bytes 10485760 | tf_op jit(solution)/shard_map/all_to_all | solution.py:368
  32.8 1442.0 %reduce-scatter.2.cloned.1.call-start = ((), (), s32[]{:S(2)}) async-start(), calls=%async_computation.4 | async-start | bytes 2621440 | tf_op jit(solution)/shard_map/reduce_scatter | solution.py:392
  1474.8 25.0 %all-to-all-start.2 = ((bf16[8,32,1024]{2,1,0:T(8,128)(2,1)}), bf16[8,32,1024]{2,1,0:T(8,128)(2,1)S(1)}, u32[]{:S(2)}, u32[]{:S(2)}) async-start(bf16[8,32,1024]{2,1,0:T(8,128)(2,1)} %reduce-scatter.2.cloned.1.call-done), calls=%async_computation.3 | async-start | bytes 1048576 | tf_op jit(solution)/shard_map/all_to_all | solution.py:398
  1481.3 19.3 %copy-start.1 = (bf16[2,16,4096]{2,1,0:T(8,128)(2,1)S(1)}, bf16[2,16,4096]{2,1,0:T(8,128)(2,1)}, u32[]{:S(2)}) copy-start(bf16[2,16,4096]{2,1,0:T(8,128)(2,1)} %param.8) | copy-start | bytes 786436
Sparse Core Ops, SparseCore 0:
  1437.6 32.9 reduce-scatter.1
